TPU v7x, 128 devices: a whole 4x4x4 slice. The times are simulated.
128 devices in a mesh: band: 8 (over z, core), mem: 16 (over x, y).
Axes of the slice: x: 4, y: 4, z: 4, core: 2. Of those that a mesh axis runs over, the one named last changes fastest.
Arguments:
- prior_ensemble: bfloat16 [1024, 262144], P('mem', 'band'), may hold values from -6 to 6
- perturbed_measurements: bfloat16 [1024, 16384], P('mem', 'band'), may hold values from -6 to 6
- solved_residuals: bfloat16 [1024, 16384], P('mem', 'band'), may hold values from -6 to 6
- localisation_matrix: float32 [8, 128, 128], replicated, may hold values from 0 to 1
- piece_owner_device: int32 [2048], P('band'), may hold values from 0 to 15, as said below
- measurement_group_matrix: int32 [2048, 6], P('band'), may hold values from 0 to 127, as said below
- localisation_factors: int32 [2048, 6], P('band'), may hold values from 0 to 7
Outputs:
- analysis: bfloat16 [1024, 262144], P('mem', 'band')
- spread: float32 [4096, 128], P(('band', 'mem'))
Inputs may be any that keep to these rules, and one draw needn't show every extreme that they name: `piece_owner_device`: within a band, no owner has more than 32 patches, and in every band one owner has exactly 32. `measurement_group_matrix`: patch p of band b = p // 256 has the centre block c = b * 16 + (p - b * 256) // 16 and uses only blocks c - 2 to c + 2.
All inputs are finite; a program needn't handle non-finite values.
Results may differ from a plain program's by a relative error of at most 0.0065.
Values may be sent and summed in bfloat16 or wider, within the bound.
A program may use at most 192 MiB of HBM per device.

v0:
```python
import functools

import jax
import jax.numpy as jnp
from jax import lax
from jax.experimental import pallas as pl
from jax.experimental.pallas import tpu as pltpu
from jax.sharding import PartitionSpec as P

RIM = 2
SPAN = 128
PAIR = 2 * SPAN
F32 = jnp.float32
BF16 = jnp.bfloat16


def pair_weights(rel, fac, table, w_ref, pair, blocks, nblk, scale):
    for half in range(2):
        base = (2 * pair + half) * nblk
        tiles = [table[fac[base + k]] for k in range(nblk)]
        for j in range(blocks):
            total = None
            for k in range(nblk):
                term = jnp.where(rel[base + k] == j, scale, 0.0) * tiles[k]
                total = term if total is None else total + term
            w_ref[pl.ds(j * SPAN, SPAN), pl.ds(half * SPAN, SPAN)] = total


def pair_update(x_ref, u_ref, var_ref, ydt, s_all, w_ref, xd, cov, gain, inc):
    members = x_ref.shape[0]
    step = 128
    rows = [pl.ds(r, step) for r in range(0, members, step)]
    total = jnp.zeros((1, PAIR), F32)
    for r in rows:
        total = total + jnp.sum(x_ref[r, :].astype(F32), axis=0, keepdims=True)
    mean = total / members
    for r in rows:
        xd[r, :] = (x_ref[r, :].astype(F32) - mean).astype(BF16)
    cov[...] = jnp.dot(ydt[...], xd[...], preferred_element_type=F32)
    for r in range(0, cov.shape[0], step):
        r = pl.ds(r, step)
        gain[r, :] = (w_ref[r, :] * cov[r, :]).astype(BF16)
    inc[...] = jnp.dot(s_all[...], gain[...], preferred_element_type=F32)
    total = jnp.zeros((1, PAIR), F32)
    for r in rows:
        new = (x_ref[r, :].astype(F32) + inc[r, :]).astype(BF16)
        u_ref[r, :] = new
        total = total + jnp.sum(new.astype(F32), axis=0, keepdims=True)
    mean = total / members
    total = jnp.zeros((1, PAIR), F32)
    for r in rows:
        off = u_ref[r, :].astype(F32) - mean
        total = total + jnp.sum(off * off, axis=0, keepdims=True)
    var_ref[...] = total / members


def prepare_obs(obs, ydt, s_all, blocks):
    members = obs[0].shape[1]
    for j in range(blocks):
        y = obs[j][0].astype(F32)
        dev = y - jnp.sum(y, axis=0, keepdims=True) / members
        ydt[pl.ds(j * SPAN, SPAN), :] = jnp.transpose(dev).astype(BF16)
        s_all[:, pl.ds(j * SPAN, SPAN)] = obs[j][1]


def update_kernel(nblk, rel, fac, table, x_ref, *refs):
    blocks = 2 * RIM + 1
    obs, (u_ref, var_ref, ydt, s_all, w_ref, xd, cov, gain, inc) = refs[:blocks], refs[blocks:]
    members = x_ref.shape[0]
    pair = pl.program_id(0)

    @pl.when(pair == 0)
    def _():
        prepare_obs(obs, ydt, s_all, blocks)

    pair_weights(rel, fac, table, w_ref, pair, blocks, nblk, 1.0 / (members - 1))
    pair_update(x_ref, u_ref, var_ref.at[0], ydt, s_all, w_ref, xd, cov, gain, inc)


def update(rel, fac, table, x, obs):
    members, width = x.shape
    blocks = 2 * RIM + 1
    nblk = rel.shape[1]
    whole = lambda *shape: pl.BlockSpec(shape, lambda i, *_: (0,) * len(shape))
    u, var = pl.pallas_call(
        functools.partial(update_kernel, nblk),
        out_shape=(
            jax.ShapeDtypeStruct(x.shape, BF16),
            jax.ShapeDtypeStruct((width // PAIR, 1, PAIR), F32),
        ),
        grid_spec=pltpu.PrefetchScalarGridSpec(
            num_scalar_prefetch=2,
            grid=(width // PAIR,),
            in_specs=[
                whole(*table.shape),
                pl.BlockSpec((members, PAIR), lambda i, *_: (0, i)),
                *[whole(2, members, SPAN)] * blocks,
            ],
            out_specs=(
                pl.BlockSpec((members, PAIR), lambda i, *_: (0, i)),
                pl.BlockSpec((1, 1, PAIR), lambda i, *_: (i, 0, 0)),
            ),
            scratch_shapes=[
                pltpu.VMEM((blocks * SPAN, members), BF16),
                pltpu.VMEM((members, blocks * SPAN), BF16),
                pltpu.VMEM((blocks * SPAN, PAIR), F32),
                pltpu.VMEM((members, PAIR), BF16),
                pltpu.VMEM((blocks * SPAN, PAIR), F32),
                pltpu.VMEM((blocks * SPAN, PAIR), BF16),
                pltpu.VMEM((members, PAIR), F32),
            ],
        ),
        compiler_params=pltpu.CompilerParams(vmem_limit_bytes=48 << 20),
    )(rel.reshape(-1), fac.reshape(-1), table, x, *obs)
    return u, var.reshape(-1, SPAN)


def per_device(prior, perturbed, solved, taper, owner, groups, factors):
    mems, bands = lax.axis_size("mem"), lax.axis_size("band")
    me, band = lax.axis_index("mem"), lax.axis_index("band")
    patches = owner.shape[0]
    per_worker = patches // mems
    capacity = 2 * per_worker
    table = jnp.transpose(taper, (0, 2, 1))
    start = me * per_worker
    centre = band * mems + me
    rel = lax.dynamic_slice_in_dim(groups, start, per_worker, 0) - centre + RIM
    fac = lax.dynamic_slice_in_dim(factors, start, per_worker, 0)

    obs = jnp.stack([perturbed, solved])
    own = lax.all_to_all(obs, "mem", split_axis=2, concat_axis=1, tiled=True)
    count = mems * bands
    near = {0: own}
    for d in (1, -1, 2, -2):
        near[d] = lax.ppermute(own, ("band", "mem"), [(i, (i - d) % count) for i in range(count)])
    x = lax.all_to_all(prior, "mem", split_axis=1, concat_axis=0, tiled=True)
    updated, variance = update(rel, fac, table, x, [near[d] for d in range(-RIM, RIM + 1)])
    analysis = lax.all_to_all(updated, "mem", split_axis=0, concat_axis=1, tiled=True)
    every = lax.all_to_all(jnp.tile(variance, (mems, 1)), "mem", split_axis=0, concat_axis=0, tiled=True)
    mine = (owner == me).astype(jnp.int32)
    rank = jnp.cumsum(mine) - mine
    slots = jnp.arange(capacity, dtype=jnp.int32)
    selector = ((rank[None, :] == slots[:, None]) & (mine[None, :] == 1)).astype(F32)
    spread = jnp.dot(selector, every, precision=lax.Precision.HIGHEST, preferred_element_type=F32)
    return analysis, spread


def solution(mesh):
    return jax.shard_map(
        per_device,
        mesh=mesh,
        in_specs=(
            P("mem", "band"),
            P("mem", "band"),
            P("mem", "band"),
            P(),
            P("band"),
            P("band", None),
            P("band", None),
        ),
        out_specs=(P("mem", "band"), P(("band", "mem"), None)),
        check_vma=False,
    )
```

profile of v0, /device:TPU:112, one launch (start us, length us, event | category | flops | bytes accessed | tf_op | source)
XLA Modules:
  0.0 214.3 jit_solution(12817268859341640807)
XLA Ops:
  0.6 1.1 pad_maximum_fusion
  1.7 0.8 copy.33
  2.5 1.5 reshape.45
  4.0 7.3 %all-to-all-start.1 = ((bf16[16,2,8192]{2,1,0:T(2,128)(2,1)}), bf16[16,2,8192]{2,1,0:T(2,128)(2,1)S(1)}, u32[]{:S(2)}, u32[]{:S(2)}) async-start(bf16[16,2,8192]{2,1,0:T(2,128)(2,1)} %reshape.45), calls=%async_computation.1 | async-start | bytes 1048576 | tf_op jit(solution)/shard_map/all_to_all | solution.py:131
  11.3 4.8 %copy.39 = bf16[8,16,8,2048]{3,2,0,1:T(8,128)(2,1)} copy(bf16[8,16,8,2048]{3,2,1,0:T(8,128)(2,1)} %bitcast.37) | data formatting | bytes 8388608 | tf_op jit(solution)/shard_map/all_to_all | solution.py:136
  16.1 4.4 %all-to-all-done.1 = bf16[16,2,8192]{2,1,0:T(2,128)(2,1)S(1)} async-done(((bf16[16,2,8192]{2,1,0:T(2,128)(2,1)}), bf16[16,2,8192]{2,1,0:T(2,128)(2,1)S(1)}, u32[]{:S(2)}, u32[]{:S(2)}) %all-to-all-start.1) | async-done | bytes 524320 | tf_op jit(solution)/shard_map/all_to_all | solution.py:131
  20.4 6.8 %all-to-all-start = ((bf16[64,16,2048]{2,0,1:T(8,128)(2,1)}), bf16[64,16,2048]{2,0,1:T(8,128)(2,1)}, u32[]{:S(2)}, u32[]{:S(2)}) async-start(bf16[64,16,2048]{2,0,1:T(8,128)(2,1)} %bitcast.34), calls=%async_computation | async-start | bytes 8388608 | tf_op jit(solution)/shard_map/all_to_all | solution.py:136
  27.3 0.7 reshape.46
  27.9 0.8 copy.34
  28.7 1.6 collective-permute-start
  30.2 2.1 collective-permute-start.1
  32.3 5.9 %collective-permute-start.3 = (bf16[2,1024,128]{2,1,0:T(8,128)(2,1)S(1)}, bf16[2,1024,128]{2,1,0:T(8,128)(2,1)S(1)}, u32[]{:S(2)}, u32[]{:S(2)}) collective-permute-start(bf16[2,1024,128]{2,1,0:T(8,128)(2,1)S(1)} %bitcast.30), channel_id=1, source_target_pairs={{0,126},{1,127},{2,0},{3,1},{4,2},{5,3},{6,4},{7,5},{8,6},{9,7},{1... | collective-permute-start | bytes 1572872 | tf_op jit(solution)/shard_map/ppermute | solution.py:135
  38.7 1.2 copy.31
  39.9 51.4 %collective-permute-done.refs_0_ = bf16[2,1024,128]{2,1,0:T(8,128)(2,1)S(1)} collective-permute-done((bf16[2,1024,128]{2,1,0:T(8,128)(2,1)S(1)}, bf16[2,1024,128]{2,1,0:T(8,128)(2,1)S(1)}, u32[]{:S(2)}, u32[]{:S(2)}) %collective-permute-start) | collective-permute-done | bytes 524320 | tf_op jit(solution)/shard_map/ppermute | solution.py:135
  91.3 5.2 %collective-permute-done.1.refs_1_ = bf16[2,1024,128]{2,1,0:T(8,128)(2,1)S(1)} collective-permute-done((bf16[2,1024,128]{2,1,0:T(8,128)(2,1)S(1)}, bf16[2,1024,128]{2,1,0:T(8,128)(2,1)S(1)}, u32[]{:S(2)}, u32[]{:S(2)}) %collective-permute-start.1) | collective-permute-done | bytes 524320 | tf_op jit(solution)/shard_map/ppermute | solution.py:135
  96.5 1.1 collective-permute-done.2.refs_3_
  97.6 14.8 %collective-permute-done.3.refs_4_ = bf16[2,1024,128]{2,1,0:T(8,128)(2,1)S(1)} collective-permute-done((bf16[2,1024,128]{2,1,0:T(8,128)(2,1)S(1)}, bf16[2,1024,128]{2,1,0:T(8,128)(2,1)S(1)}, u32[]{:S(2)}, u32[]{:S(2)}) %collective-permute-start.3) | collective-permute-done | bytes 524320 | tf_op jit(solution)/shard_map/ppermute | solution.py:135
  112.4 18.7 %shard_map.86 = (bf16[1024,2048]{1,0:T(8,128)(2,1)}, f32[8,1,256]{2,1,0:T(1,128)S(1)}) custom-call(s32[96]{0:T(128)S(1)} %reshape.40.rel, s32[96]{0:T(128)S(1)} %reshape.41.fac, f32[8,128,128]{2,1,0:T(8,128)S(1)} %bitcast.32, bf16[1024,2048]{1,0:T(8,128)(2,1)} %bitcast.2.x_ref, bf16[2,1024,128]{2,1,0:T(8,128)(2,1)S(1)} %collective-permute-done.refs_0_, ...), custom_call_target="tpu_custom_call" | custom-call | tf_op jit(solution)/shard_map/pallas_call | solution.py:85
  131.2 21.8 %all_to_all.65 = f32[16,16,128]{2,1,0:T(8,128)S(1)} all-to-all(f32[16,16,128]{2,1,0:T(8,128)S(1)} %tile.9), channel_id=1, replica_groups=mesh['band'=8,'mem'=16] {'mem'}, dimensions={0} | all-to-all | bytes 262144 | tf_op jit(solution)/shard_map/all_to_all | solution.py:139
  152.9 6.4 %all-to-all-start.2 = ((bf16[16,64,2048]{2,1,0:T(8,128)(2,1)}), bf16[16,64,2048]{2,1,0:T(8,128)(2,1)}, u32[]{:S(2)}, u32[]{:S(2)}) async-start(bf16[16,64,2048]{2,1,0:T(8,128)(2,1)} %bitcast.38), calls=%async_computation.2 | async-start | bytes 8388608 | tf_op jit(solution)/shard_map/all_to_all | solution.py:138
  159.4 0.3 reduce-window.9
  160.0 0.8 fusion.1
  160.8 48.8 %all-to-all-done.2 = bf16[16,64,2048]{2,1,0:T(8,128)(2,1)} async-done(((bf16[16,64,2048]{2,1,0:T(8,128)(2,1)}), bf16[16,64,2048]{2,1,0:T(8,128)(2,1)}, u32[]{:S(2)}, u32[]{:S(2)}) %all-to-all-start.2) | async-done | bytes 4194336 | tf_op jit(solution)/shard_map/all_to_all | solution.py:138
  209.6 4.8 %copy.37 = bf16[16,8,8,2048]{3,2,0,1:T(8,128)(2,1)} copy(bf16[16,8,8,2048]{3,2,1,0:T(8,128)(2,1)} %bitcast.18) | data formatting | bytes 8388608 | tf_op jit(solution)/shard_map/all_to_all | solution.py:138
  (19 shorter events, 0.8 us)
Async XLA Ops:
  4.0 16.5 %all-to-all-start.1 = ((bf16[16,2,8192]{2,1,0:T(2,128)(2,1)}), bf16[16,2,8192]{2,1,0:T(2,128)(2,1)S(1)}, u32[]{:S(2)}, u32[]{:S(2)}) async-start(bf16[16,2,8192]{2,1,0:T(2,128)(2,1)} %reshape.45), calls=%async_computation.1 | async-start | bytes 1048576 | tf_op jit(solution)/shard_map/all_to_all | solution.py:131
  20.4 17.8 %copy-start.1 = (s32[256,6]{0,1:T(8,128)S(1)}, s32[256,6]{0,1:T(8,128)}, u32[]{:S(2)}) copy-start(s32[256,6]{0,1:T(8,128)} %param.12) | copy-start | bytes 18436
  20.4 17.8 %copy-start.2 = (s32[256,6]{0,1:T(8,128)S(1)}, s32[256,6]{0,1:T(8,128)}, u32[]{:S(2)}) copy-start(s32[256,6]{0,1:T(8,128)} %param.13) | copy-start | bytes 18436
  20.4 92.0 %all-to-all-start = ((bf16[64,16,2048]{2,0,1:T(8,128)(2,1)}), bf16[64,16,2048]{2,0,1:T(8,128)(2,1)}, u32[]{:S(2)}, u32[]{:S(2)}) async-start(bf16[64,16,2048]{2,0,1:T(8,128)(2,1)} %bitcast.34), calls=%async_computation | async-start | bytes 8388608 | tf_op jit(solution)/shard_map/all_to_all | solution.py:136
  28.7 62.6 %collective-permute-start = (bf16[2,1024,128]{2,1,0:T(8,128)(2,1)S(1)}, bf16[2,1024,128]{2,1,0:T(8,128)(2,1)S(1)}, u32[]{:S(2)}, u32[]{:S(2)}) collective-permute-start(bf16[2,1024,128]{2,1,0:T(8,128)(2,1)S(1)} %bitcast.27), channel_id=1, source_target_pairs={{0,2},{1,3},{2,4},{3,5},{4,6},{5,7},{6,8},{7,9},{8,10},{9,11},{10,... | collective-permute-start | bytes 1572872 | tf_op jit(solution)/shard_map/ppermute | solution.py:135
  30.2 66.3 %collective-permute-start.1 = (bf16[2,1024,128]{2,1,0:T(8,128)(2,1)S(1)}, bf16[2,1024,128]{2,1,0:T(8,128)(2,1)S(1)}, u32[]{:S(2)}, u32[]{:S(2)}) collective-permute-start(bf16[2,1024,128]{2,1,0:T(8,128)(2,1)S(1)} %bitcast.28), channel_id=1, source_target_pairs={{0,1},{1,2},{2,3},{3,4},{4,5},{5,6},{6,7},{7,8},{8,9},{9,10},{10,1... | collective-permute-start | bytes 1572872 | tf_op jit(solution)/shard_map/ppermute | solution.py:135
  32.3 65.3 %collective-permute-start.2 = (bf16[2,1024,128]{2,1,0:T(8,128)(2,1)S(1)}, bf16[2,1024,128]{2,1,0:T(8,128)(2,1)S(1)}, u32[]{:S(2)}, u32[]{:S(2)}) collective-permute-start(bf16[2,1024,128]{2,1,0:T(8,128)(2,1)S(1)} %bitcast.29), channel_id=1, source_target_pairs={{0,127},{1,0},{2,1},{3,2},{4,3},{5,4},{6,5},{7,6},{8,7},{9,8},{10,... | collective-permute-start | bytes 1572872 | tf_op jit(solution)/shard_map/ppermute | solution.py:135
  32.3 80.1 %collective-permute-start.3 = (bf16[2,1024,128]{2,1,0:T(8,128)(2,1)S(1)}, bf16[2,1024,128]{2,1,0:T(8,128)(2,1)S(1)}, u32[]{:S(2)}, u32[]{:S(2)}) collective-permute-start(bf16[2,1024,128]{2,1,0:T(8,128)(2,1)S(1)} %bitcast.30), channel_id=1, source_target_pairs={{0,126},{1,127},{2,0},{3,1},{4,2},{5,3},{6,4},{7,5},{8,6},{9,7},{1... | collective-permute-start | bytes 1572872 | tf_op jit(solution)/shard_map/ppermute | solution.py:135
  152.9 6.4 %copy-start = (s32[256]{0:T(256)S(1)}, s32[256]{0:T(256)}, u32[]{:S(2)}) copy-start(s32[256]{0:T(256)} %param.11) | copy-start | bytes 3076
  152.9 56.6 %all-to-all-start.2 = ((bf16[16,64,2048]{2,1,0:T(8,128)(2,1)}), bf16[16,64,2048]{2,1,0:T(8,128)(2,1)}, u32[]{:S(2)}, u32[]{:S(2)}) async-start(bf16[16,64,2048]{2,1,0:T(8,128)(2,1)} %bitcast.38), calls=%async_computation.2 | async-start | bytes 8388608 | tf_op jit(solution)/shard_map/all_to_all | solution.py:138
where the time goes:
time: 215 us; the launch traced here: 214 us
  waiting for transfers between devices  126 us (59%)
  starting transfers between devices  30.1 us (14%)
  blocking collectives  21.8 us (10%)
  Pallas kernels  18.7 us (9%)
  local copies, waits for them, and re-layouts  15.1 us (7%)
    ppermute x4, waiting for transfers between devices, per_device(): lax.ppermute(own, ('band', 'mem'), [(i, (i - d) % count) for i in range(c...  72.5 us
    all_to_all x1, waiting for transfers between devices, per_device(): lax.all_to_all(updated, 'mem', split_axis=0, concat_axis=1, tiled=True)  48.8 us
    all_to_all x1, blocking collectives, per_device(): lax.all_to_all(jnp.tile(variance, (mems, 1)), 'mem', split_axis=0, concat...  21.8 us
    pallas_call x1, Pallas kernels, update(): pl.pallas_call(functools.partial(update_kernel, nblk), out_shape=(jax.Sha...  18.7 us
    ppermute x4, starting transfers between devices, per_device(): lax.ppermute(own, ('band', 'mem'), [(i, (i - d) % count) for i in range(c...  9.57 us
    all_to_all x1, starting transfers between devices, per_device(): own = lax.all_to_all(obs, 'mem', split_axis=2, concat_axis=1, tiled=True)  7.28 us
    all_to_all x1, starting transfers between devices, per_device(): x = lax.all_to_all(prior, 'mem', split_axis=1, concat_axis=0, tiled=True)  6.82 us
    all_to_all x1, starting transfers between devices, per_device(): lax.all_to_all(updated, 'mem', split_axis=0, concat_axis=1, tiled=True)  6.42 us
  transfers between devices with their start and end apart: 7, of which 6 were waited for; matrix products, arithmetic and copies ran while one was open for 4% of the time, Pallas kernels for 0%

commit v1 on v0

v1 whole, which is shorter than its diff:
```python
import functools

import jax
import jax.numpy as jnp
from jax import lax
from jax.experimental import pallas as pl
from jax.experimental.pallas import tpu as pltpu
from jax.sharding import PartitionSpec as P

RIM = 2
BLOCKS = 2 * RIM + 1
SPAN = 128
PAIR = 2 * SPAN
SIDE = 4
F32 = jnp.float32
BF16 = jnp.bfloat16
MESH = pl.DeviceIdType.MESH
HOPS = ((0, 1), (1, 0), (0, 3), (3, 0), (1, 1), (3, 3), (1, 3), (3, 1), (0, 2), (2, 0), (1, 2), (2, 1), (3, 2), (2, 3), (2, 2))


def pair_weights(rel, fac, table, w_ref, pair, nblk, scale):
    for half in range(2):
        base = (2 * pair + half) * nblk
        tiles = [table[fac[base + k]] for k in range(nblk)]
        for j in range(BLOCKS):
            total = None
            for k in range(nblk):
                term = jnp.where(rel[base + k] == j, scale, 0.0) * tiles[k]
                total = term if total is None else total + term
            w_ref[pl.ds(j * SPAN, SPAN), pl.ds(half * SPAN, SPAN)] = total


def pair_update(x_ref, u_ref, ydt, s_all, w_ref, xd, cov, gain, inc):
    members = x_ref.shape[0]
    step = 128
    rows = [pl.ds(r, step) for r in range(0, members, step)]
    total = jnp.zeros((1, PAIR), F32)
    for r in rows:
        total = total + jnp.sum(x_ref[r, :].astype(F32), axis=0, keepdims=True)
    mean = total / members
    for r in rows:
        xd[r, :] = (x_ref[r, :].astype(F32) - mean).astype(BF16)
    cov[...] = jnp.dot(ydt[...], xd[...], preferred_element_type=F32)
    for r in range(0, cov.shape[0], step):
        r = pl.ds(r, step)
        gain[r, :] = (w_ref[r, :] * cov[r, :]).astype(BF16)
    inc[...] = jnp.dot(s_all[...], gain[...], preferred_element_type=F32)
    total = jnp.zeros((1, PAIR), F32)
    for r in rows:
        new = (x_ref[r, :].astype(F32) + inc[r, :]).astype(BF16)
        u_ref[r, :] = new
        total = total + jnp.sum(new.astype(F32), axis=0, keepdims=True)
    mean = total / members
    total = jnp.zeros((1, PAIR), F32)
    for r in rows:
        off = u_ref[r, :].astype(F32) - mean
        total = total + jnp.sum(off * off, axis=0, keepdims=True)
    return total / members


def place(band, w):
    return w


def kernel(
    nblk, mems, bands,
    rel, fac, table, owner, prior, perturbed, solved,
    out, spread,
    xbuf, ubuf, obs, ydt, s_all, weights, xd, cov, gain, inc, var_mine, var_all,
    own_sem, own_send, near_recv, near_send, in_recv, in_send, out_recv, out_send, var_recv, var_send,
):
    band, me = lax.axis_index("band"), lax.axis_index("mem")
    x, y = me // SIDE, me % SIDE
    worker = place(band, me)
    members = xbuf.shape[1]
    local = prior.shape[0]
    pairs = xbuf.shape[0]
    width = pairs * PAIR
    peers = [((x + dx) % SIDE) * SIDE + (y + dy) % SIDE for dx, dy in HOPS]
    rows = pl.ds(pl.multiple_of(me * local, local), local)

    def chain(step):
        g = (band * mems + worker + step + bands * mems) % (bands * mems)
        return {"band": g // mems, "mem": place(g // mems, g % mems)}

    right, left = chain(1), chain(-1)

    barrier = pltpu.get_barrier_semaphore()
    for peer in peers:
        pl.semaphore_signal(barrier, inc=1, device_id={"mem": peer}, device_id_type=MESH)
    for peer in (left, right):
        pl.semaphore_signal(barrier, inc=1, device_id=peer, device_id_type=MESH)
    pl.semaphore_wait(barrier, len(peers) + 2)

    def columns(w, pair):
        return pl.ds(pl.multiple_of(w * width + pair * PAIR, PAIR), PAIR)

    def all_of(ref, sem):
        return pltpu.make_async_copy(ref, ref, sem)

    for i, source in enumerate((perturbed, solved)):
        pltpu.make_async_copy(
            source.at[:, pl.ds(pl.multiple_of(worker * SPAN, SPAN), SPAN)], obs.at[RIM, i, rows, :], own_sem
        ).start()
        for peer in peers:
            w = place(band, peer)
            pltpu.make_async_remote_copy(
                source.at[:, pl.ds(pl.multiple_of(w * SPAN, SPAN), SPAN)],
                obs.at[RIM, i, rows, :],
                own_send, own_sem, device_id={"mem": peer}, device_id_type=MESH,
            ).start()

    def send_prior(pair, carry):
        pltpu.make_async_copy(prior.at[:, columns(worker, pair)], xbuf.at[pair, rows, :], in_recv.at[pair]).start()
        for peer in peers:
            pltpu.make_async_remote_copy(
                prior.at[:, columns(place(band, peer), pair)], xbuf.at[pair, rows, :],
                in_send, in_recv.at[pair], device_id={"mem": peer}, device_id_type=MESH,
            ).start()
        return carry

    def make_weights(pair, carry):
        pair_weights(rel, fac, table, weights.at[pair], pair, nblk, 1.0 / (members - 1))
        return carry

    def near_copy(source, target, slot, i, peer):
        return pltpu.make_async_remote_copy(
            obs.at[source, i], obs.at[target, i],
            near_send.at[slot, i], near_recv.at[slot, i], device_id=peer, device_id_type=MESH,
        )

    lax.fori_loop(0, 2, send_prior, 0)
    lax.fori_loop(0, 2, make_weights, 0)
    all_of(obs.at[RIM], own_sem).wait()
    first = [(near_copy(2, 1, 0, i, right), near_copy(2, 3, 1, i, left)) for i in range(2)]
    second = [(near_copy(1, 0, 2, i, right), near_copy(3, 4, 3, i, left)) for i in range(2)]
    for pair_of in first:
        for copy in pair_of:
            copy.start()
    lax.fori_loop(2, 4, send_prior, 0)
    lax.fori_loop(2, 4, make_weights, 0)
    for pair_of, onward in zip(first, second):
        for copy, relay in zip(pair_of, onward):
            copy.wait_recv()
            relay.start()
    lax.fori_loop(4, pairs, send_prior, 0)
    lax.fori_loop(4, pairs, make_weights, 0)
    for pair_of in second:
        for copy in pair_of:
            copy.wait_recv()

    for j in range(BLOCKS):
        block = obs[j, 0].astype(F32)
        dev = block - jnp.sum(block, axis=0, keepdims=True) / members
        ydt[pl.ds(j * SPAN, SPAN), :] = jnp.transpose(dev).astype(BF16)
        s_all[:, pl.ds(j * SPAN, SPAN)] = obs[j, 1]

    def update(pair, carry):
        all_of(xbuf.at[pair], in_recv.at[pair]).wait()
        var = pair_update(xbuf.at[pair], ubuf.at[pair], ydt, s_all, weights.at[pair], xd, cov, gain, inc)
        var_mine[pl.ds(pair, 1), :] = var
        target = columns(worker, pair)
        pltpu.make_async_copy(ubuf.at[pair, rows, :], out.at[:, target], out_recv).start()
        for peer in peers:
            theirs = pl.ds(pl.multiple_of(peer * local, local), local)
            pltpu.make_async_remote_copy(
                ubuf.at[pair, theirs, :], out.at[:, target],
                out_send, out_recv, device_id={"mem": peer}, device_id_type=MESH,
            ).start()
        return carry

    lax.fori_loop(0, pairs, update, 0)

    pltpu.make_async_copy(var_mine, var_all.at[worker], var_recv).start()
    for peer in peers:
        pltpu.make_async_remote_copy(
            var_mine, var_all.at[worker], var_send, var_recv, device_id={"mem": peer}, device_id_type=MESH
        ).start()

    mine = jnp.where(owner[...] == me, 1.0, 0.0).astype(F32)
    even, odd = mine[0:1, :], mine[1:2, :]
    count = even.shape[1]
    before = (
        lax.broadcasted_iota(jnp.int32, (count, count), 0) < lax.broadcasted_iota(jnp.int32, (count, count), 1)
    )
    rank = jnp.dot(
        jnp.broadcast_to(even + odd, (8, count)).astype(BF16),
        jnp.where(before, 1.0, 0.0).astype(BF16),
        preferred_element_type=F32,
    )[0:1, :]
    slots = lax.broadcasted_iota(jnp.int32, (spread.shape[0], count), 0).astype(F32)
    all_of(var_all, var_recv).wait()
    total = None
    for half, (hit, order) in enumerate(((even, rank), (odd, rank + even))):
        selector = jnp.where(slots == order, 1.0, 0.0) * hit
        values = var_all[:, :, pl.ds(half * SPAN, SPAN)].reshape(count, SPAN)
        term = jnp.dot(selector, values, precision=lax.Precision.HIGHEST, preferred_element_type=F32)
        total = term if total is None else total + term
    spread[...] = total

    for pair_of in first + second:
        for copy in pair_of:
            copy.wait_send()
    part = xbuf.at[:, pl.ds(0, members - local), :]
    all_of(obs.at[RIM, :, pl.ds(0, members - local), :], own_send).wait()
    all_of(part, in_send).wait()
    all_of(var_all.at[pl.ds(0, mems - 1)], var_send).wait()
    all_of(part, out_send).wait()
    all_of(out, out_recv).wait()


def per_device(prior, perturbed, solved, taper, owner, groups, factors):
    mems, bands = lax.axis_size("mem"), lax.axis_size("band")
    me, band = lax.axis_index("mem"), lax.axis_index("band")
    local, span = prior.shape
    members = local * mems
    patches, nblk = groups.shape
    per_worker = patches // mems
    pairs = per_worker // 2
    capacity = 2 * per_worker
    worker = place(band, me)
    table = jnp.transpose(taper, (0, 2, 1))
    start = worker * per_worker
    rel = lax.dynamic_slice_in_dim(groups, start, per_worker, 0) - (band * mems + worker) + RIM
    fac = lax.dynamic_slice_in_dim(factors, start, per_worker, 0)
    vmem = pl.BlockSpec(memory_space=pltpu.VMEM)
    smem = pl.BlockSpec(memory_space=pltpu.SMEM)
    hbm = pl.BlockSpec(memory_space=OUT_SPACE)
    rim = BLOCKS * SPAN
    dma = pltpu.SemaphoreType.DMA
    return pl.pallas_call(
        functools.partial(kernel, nblk, mems, bands),
        out_shape=(
            jax.ShapeDtypeStruct(prior.shape, BF16),
            jax.ShapeDtypeStruct((capacity, SPAN), F32),
        ),
        in_specs=[smem, smem, vmem, vmem] + [pl.BlockSpec(memory_space=pltpu.HBM)] * 3,
        out_specs=(hbm, vmem),
        scratch_shapes=[
            pltpu.VMEM((pairs, members, PAIR), BF16),
            pltpu.VMEM((pairs, members, PAIR), BF16),
            pltpu.VMEM((BLOCKS, 2, members, SPAN), BF16),
            pltpu.VMEM((rim, members), BF16),
            pltpu.VMEM((members, rim), BF16),
            pltpu.VMEM((pairs, rim, PAIR), F32),
            pltpu.VMEM((members, PAIR), BF16),
            pltpu.VMEM((rim, PAIR), F32),
            pltpu.VMEM((rim, PAIR), BF16),
            pltpu.VMEM((members, PAIR), F32),
            pltpu.VMEM((pairs, PAIR), F32),
            pltpu.VMEM((mems, pairs, PAIR), F32),
            dma, dma, dma((4, 2)), dma((4, 2)), dma((pairs,)), dma, dma, dma, dma, dma,
        ],
        compiler_params=pltpu.CompilerParams(
            collective_id=0, has_side_effects=True, vmem_limit_bytes=60 << 20
        ),
    )(
        rel.reshape(-1), fac.reshape(-1), table,
        jnp.transpose(owner.reshape(patches // 2, 2)), prior, perturbed, solved,
    )


OUT_SPACE = pltpu.HBM


def solution(mesh):
    return jax.shard_map(
        per_device,
        mesh=mesh,
        in_specs=(
            P("mem", "band"),
            P("mem", "band"),
            P("mem", "band"),
            P(),
            P("band"),
            P("band", None),
            P("band", None),
        ),
        out_specs=(P("mem", "band"), P(("band", "mem"), None)),
        check_vma=False,
    )
```

time: 215 us -> 158 us (0.73)
  Pallas kernels: 18.7 us -> 145 us
  waiting for transfers between devices: 126 us -> 0 us
  starting transfers between devices: 30.1 us -> 0 us
  blocking collectives: 21.8 us -> 0 us
  local copies, waits for them, and re-layouts: 15.1 us -> 10 us
    pallas_call x1, Pallas kernels: 18.7 us -> 145 us  [per_device(): pl.pallas_call(functools.partial(kernel, nblk, mems, bands), out_shape=(j...]
    ppermute x4 -> x0, waiting for transfers between devices: 72.5 us -> none  [per_device(): lax.ppermute(own, ('band', 'mem'), [(i, (i - d) % count) for i in range(c...]
    all_to_all x3 -> x0, waiting for transfers between devices: 53.2 us -> none  [the longest x1 48.8 us: per_device(): lax.all_to_all(updated, 'mem', split_axis=0, concat_axis=1, tiled=True)]
    all_to_all x1 -> x0, blocking collectives: 21.8 us -> none  [per_device(): lax.all_to_all(jnp.tile(variance, (mems, 1)), 'mem', split_axis=0, concat...]
    all_to_all x3 -> x0, starting transfers between devices: 20.5 us -> none  [the longest x1 7.28 us: per_device(): own = lax.all_to_all(obs, 'mem', split_axis=2, concat_axis=1, tiled=True)]
    all_to_all x3 -> x0, local copies, waits for them, and re-layouts: 10.3 us -> none  [the longest x1 4.79 us: per_device(): lax.all_to_all(updated, 'mem', split_axis=0, concat_axis=1, tiled=True)]
    ppermute x4 -> x0, starting transfers between devices: 9.57 us -> none  [per_device(): lax.ppermute(own, ('band', 'mem'), [(i, (i - d) % count) for i in range(c...]
    unnamed x9 -> x5, local copies, waits for them, and re-layouts: 3.41 us -> 7.12 us
  transfers between devices with their start and end apart: 7 -> 0, of which waited for: 6 -> 0; matrix products, arithmetic and copies ran while one was open for 4% -> 0% of each run, Pallas kernels for 0% -> 0%
where the time goes in v1:
time: 158 us; the launch traced here: 156 us
  Pallas kernels  145 us (92%)
  local copies, waits for them, and re-layouts  10 us (6%)
    pallas_call x1, Pallas kernels, per_device(): pl.pallas_call(functools.partial(kernel, nblk, mems, bands), out_shape=(j...  145 us
    unnamed x5, local copies, waits for them, and re-layouts  7.12 us

profile of v1, /device:TPU:112, one launch (start us, length us, event | category | flops | bytes accessed | tf_op | source)
XLA Modules:
  0.0 156.1 jit_solution(7280440161352309292)
XLA Ops:
  0.6 0.8 subtract_add_fusion
  1.4 0.1 copy.12
  1.5 0.6 reshape.13.rel
  2.1 0.1 copy.13
  2.2 0.7 reshape.14.fac
  2.9 0.8 reshape.15
  3.7 0.6 copy.15
  4.3 2.0 %copy.14 = f32[8,128,128]{1,2,0:T(8,128)} copy(f32[8,128,128]{2,1,0:T(8,128)} %param.10) | data formatting | bytes 1048576 | tf_op args[3]
  6.3 144.6 %shard_map.86 = (bf16[64,32768]{1,0:T(8,128)(2,1)}, f32[32,128]{1,0:T(8,128)}) custom-call(s32[96]{0:T(128)} %reshape.13.rel, s32[96]{0:T(128)} %reshape.14.fac, f32[8,128,128]{2,1,0:T(8,128)} %bitcast.2, s32[2,128]{1,0:T(2,128)} %bitcast.3, bf16[64,32768]{1,0:T(8,128)(2,1)} %prior.1, bf16[64,2048]{1,0:T(8,128)(2,1)} %perturbed.1, bf16[64,2048]{1,0:T(8,128)(2,1)} %solved.1), custom_call_target="tpu_custom_call" | custom-call | tf_op jit(solution)/shard_map/pallas_call | solution.py:231
  151.0 0.0 copy-start
  151.0 4.5 %copy.18 = bf16[64,32768]{1,0:T(8,128)(2,1)} copy(bf16[64,32768]{1,0:T(8,128)(2,1)} %get-tuple-element.6) | data formatting | bytes 8388608
  155.5 0.0 copy-done
  155.5 0.6 copy.19
Async XLA Ops:
  151.0 4.5 %copy-start = (f32[32,128]{1,0:T(8,128)S(1)}, f32[32,128]{1,0:T(8,128)}, u32[]{:S(2)}) copy-start(f32[32,128]{1,0:T(8,128)} %get-tuple-element.7) | copy-start | bytes 49156

commit v2 on v1

--- a/solution.py
+++ b/solution.py
@@ -12,20 +12,21 @@
 SPAN = 128
 PAIR = 2 * SPAN
 SIDE = 4
+CHUNK = 128
 F32 = jnp.float32
 BF16 = jnp.bfloat16
 MESH = pl.DeviceIdType.MESH
 HOPS = ((0, 1), (1, 0), (0, 3), (3, 0), (1, 1), (3, 3), (1, 3), (3, 1), (0, 2), (2, 0), (1, 2), (2, 1), (3, 2), (2, 3), (2, 2))
 
 
-def pair_weights(rel, fac, table, w_ref, pair, nblk, scale):
+def pair_weights(groups, factors, table, w_ref, patch, first, scale):
+    nblk = groups.shape[0]
     for half in range(2):
-        base = (2 * pair + half) * nblk
-        tiles = [table[fac[base + k]] for k in range(nblk)]
+        tiles = [table[factors[k, patch + half]] for k in range(nblk)]
         for j in range(BLOCKS):
             total = None
             for k in range(nblk):
-                term = jnp.where(rel[base + k] == j, scale, 0.0) * tiles[k]
+                term = jnp.where(groups[k, patch + half] == first + j, scale, 0.0) * tiles[k]
                 total = term if total is None else total + term
             w_ref[pl.ds(j * SPAN, SPAN), pl.ds(half * SPAN, SPAN)] = total
 
@@ -58,20 +59,29 @@
     return total / members
 
 
-def place(band, w):
-    return w
+def mem_of(band, w):
+    row = w // SIDE
+    along = (w % SIDE - row + SIDE) % SIDE
+    odd = band % 2
+    return (1 - odd) * (row * SIDE + along) + odd * (along * SIDE + row)
+
+
+def worker_of(band, mem):
+    x, y = mem // SIDE, mem % SIDE
+    odd = band % 2
+    return ((1 - odd) * x + odd * y) * SIDE + (x + y) % SIDE
 
 
 def kernel(
-    nblk, mems, bands,
-    rel, fac, table, owner, prior, perturbed, solved,
+    mems, bands,
+    groups, factors, taper, owner, prior, perturbed, solved,
     out, spread,
-    xbuf, ubuf, obs, ydt, s_all, weights, xd, cov, gain, inc, var_mine, var_all,
+    xbuf, ubuf, obs, table, ydt, s_all, weights, xd, cov, gain, inc, var_mine, var_all,
     own_sem, own_send, near_recv, near_send, in_recv, in_send, out_recv, out_send, var_recv, var_send,
 ):
     band, me = lax.axis_index("band"), lax.axis_index("mem")
     x, y = me // SIDE, me % SIDE
-    worker = place(band, me)
+    worker = worker_of(band, me)
     members = xbuf.shape[1]
     local = prior.shape[0]
     pairs = xbuf.shape[0]
@@ -81,7 +91,7 @@
 
     def chain(step):
         g = (band * mems + worker + step + bands * mems) % (bands * mems)
-        return {"band": g // mems, "mem": place(g // mems, g % mems)}
+        return {"band": g // mems, "mem": mem_of(g // mems, g % mems)}
 
     right, left = chain(1), chain(-1)
 
@@ -103,7 +113,7 @@
             source.at[:, pl.ds(pl.multiple_of(worker * SPAN, SPAN), SPAN)], obs.at[RIM, i, rows, :], own_sem
         ).start()
         for peer in peers:
-            w = place(band, peer)
+            w = worker_of(band, peer)
             pltpu.make_async_remote_copy(
                 source.at[:, pl.ds(pl.multiple_of(w * SPAN, SPAN), SPAN)],
                 obs.at[RIM, i, rows, :],
@@ -114,40 +124,64 @@
         pltpu.make_async_copy(prior.at[:, columns(worker, pair)], xbuf.at[pair, rows, :], in_recv.at[pair]).start()
         for peer in peers:
             pltpu.make_async_remote_copy(
-                prior.at[:, columns(place(band, peer), pair)], xbuf.at[pair, rows, :],
+                prior.at[:, columns(worker_of(band, peer), pair)], xbuf.at[pair, rows, :],
                 in_send, in_recv.at[pair], device_id={"mem": peer}, device_id_type=MESH,
             ).start()
         return carry
 
     def make_weights(pair, carry):
-        pair_weights(rel, fac, table, weights.at[pair], pair, nblk, 1.0 / (members - 1))
-        return carry
-
-    def near_copy(source, target, slot, i, peer):
+        pair_weights(
+            groups, factors, table, weights.at[pair], 2 * (worker * pairs + pair),
+            band * mems + worker - RIM, 1.0 / (members - 1),
+        )
+        return carry
+
+    def near_copy(source, target, slot, c, peer):
+        piece = pl.ds(pl.multiple_of((c % chunks) * CHUNK, CHUNK), CHUNK)
         return pltpu.make_async_remote_copy(
-            obs.at[source, i], obs.at[target, i],
-            near_send.at[slot, i], near_recv.at[slot, i], device_id=peer, device_id_type=MESH,
+            obs.at[source, c // chunks, piece, :], obs.at[target, c // chunks, piece, :],
+            near_send.at[slot, c], near_recv.at[slot, c], device_id=peer, device_id_type=MESH,
         )
 
+    chunks = members // CHUNK
+    steps = (
+        lambda c: near_copy(2, 1, 0, c, right), lambda c: near_copy(2, 3, 1, c, left),
+        lambda c: near_copy(1, 0, 2, c, right), lambda c: near_copy(3, 4, 3, c, left),
+    )
+
+    def near_first(c, carry):
+        steps[0](c).start()
+        steps[1](c).start()
+        return carry
+
+    def near_relay(c, carry):
+        for side in range(2):
+            steps[side](c).wait_recv()
+            steps[2 + side](c).start()
+        return carry
+
+    def near_last(c, carry):
+        steps[2](c).wait_recv()
+        steps[3](c).wait_recv()
+        return carry
+
+    def near_sent(c, carry):
+        for step in steps:
+            step(c).wait_send()
+        return carry
+
     lax.fori_loop(0, 2, send_prior, 0)
+    for t in range(table.shape[0]):
+        table[t] = jnp.transpose(taper[t])
     lax.fori_loop(0, 2, make_weights, 0)
     all_of(obs.at[RIM], own_sem).wait()
-    first = [(near_copy(2, 1, 0, i, right), near_copy(2, 3, 1, i, left)) for i in range(2)]
-    second = [(near_copy(1, 0, 2, i, right), near_copy(3, 4, 3, i, left)) for i in range(2)]
-    for pair_of in first:
-        for copy in pair_of:
-            copy.start()
+    lax.fori_loop(0, 2 * chunks, near_first, 0)
     lax.fori_loop(2, 4, send_prior, 0)
     lax.fori_loop(2, 4, make_weights, 0)
-    for pair_of, onward in zip(first, second):
-        for copy, relay in zip(pair_of, onward):
-            copy.wait_recv()
-            relay.start()
+    lax.fori_loop(0, 2 * chunks, near_relay, 0)
     lax.fori_loop(4, pairs, send_prior, 0)
     lax.fori_loop(4, pairs, make_weights, 0)
-    for pair_of in second:
-        for copy in pair_of:
-            copy.wait_recv()
+    lax.fori_loop(0, 2 * chunks, near_last, 0)
 
     for j in range(BLOCKS):
         block = obs[j, 0].astype(F32)
@@ -158,7 +192,8 @@
     def update(pair, carry):
         all_of(xbuf.at[pair], in_recv.at[pair]).wait()
         var = pair_update(xbuf.at[pair], ubuf.at[pair], ydt, s_all, weights.at[pair], xd, cov, gain, inc)
-        var_mine[pl.ds(pair, 1), :] = var
+        for half in range(2):
+            var_mine[pl.ds(2 * pair + half, 1), :] = var[:, half * SPAN:(half + 1) * SPAN]
         target = columns(worker, pair)
         pltpu.make_async_copy(ubuf.at[pair, rows, :], out.at[:, target], out_recv).start()
         for peer in peers:
@@ -178,29 +213,23 @@
         ).start()
 
     mine = jnp.where(owner[...] == me, 1.0, 0.0).astype(F32)
-    even, odd = mine[0:1, :], mine[1:2, :]
-    count = even.shape[1]
+    count = mine.shape[1]
     before = (
         lax.broadcasted_iota(jnp.int32, (count, count), 0) < lax.broadcasted_iota(jnp.int32, (count, count), 1)
     )
     rank = jnp.dot(
-        jnp.broadcast_to(even + odd, (8, count)).astype(BF16),
+        jnp.broadcast_to(mine, (8, count)).astype(BF16),
         jnp.where(before, 1.0, 0.0).astype(BF16),
         preferred_element_type=F32,
     )[0:1, :]
     slots = lax.broadcasted_iota(jnp.int32, (spread.shape[0], count), 0).astype(F32)
+    selector = jnp.where(slots == rank, 1.0, 0.0) * mine
     all_of(var_all, var_recv).wait()
-    total = None
-    for half, (hit, order) in enumerate(((even, rank), (odd, rank + even))):
-        selector = jnp.where(slots == order, 1.0, 0.0) * hit
-        values = var_all[:, :, pl.ds(half * SPAN, SPAN)].reshape(count, SPAN)
-        term = jnp.dot(selector, values, precision=lax.Precision.HIGHEST, preferred_element_type=F32)
-        total = term if total is None else total + term
-    spread[...] = total
-
-    for pair_of in first + second:
-        for copy in pair_of:
-            copy.wait_send()
+    spread[...] = jnp.dot(
+        selector, var_all[...].reshape(count, SPAN), precision=lax.Precision.HIGHEST, preferred_element_type=F32
+    )
+
+    lax.fori_loop(0, 2 * chunks, near_sent, 0)
     part = xbuf.at[:, pl.ds(0, members - local), :]
     all_of(obs.at[RIM, :, pl.ds(0, members - local), :], own_send).wait()
     all_of(part, in_send).wait()
@@ -211,25 +240,19 @@
 
 def per_device(prior, perturbed, solved, taper, owner, groups, factors):
     mems, bands = lax.axis_size("mem"), lax.axis_size("band")
-    me, band = lax.axis_index("mem"), lax.axis_index("band")
-    local, span = prior.shape
+    local = prior.shape[0]
     members = local * mems
-    patches, nblk = groups.shape
+    patches = owner.shape[0]
     per_worker = patches // mems
     pairs = per_worker // 2
     capacity = 2 * per_worker
-    worker = place(band, me)
-    table = jnp.transpose(taper, (0, 2, 1))
-    start = worker * per_worker
-    rel = lax.dynamic_slice_in_dim(groups, start, per_worker, 0) - (band * mems + worker) + RIM
-    fac = lax.dynamic_slice_in_dim(factors, start, per_worker, 0)
     vmem = pl.BlockSpec(memory_space=pltpu.VMEM)
     smem = pl.BlockSpec(memory_space=pltpu.SMEM)
     hbm = pl.BlockSpec(memory_space=OUT_SPACE)
     rim = BLOCKS * SPAN
     dma = pltpu.SemaphoreType.DMA
     return pl.pallas_call(
-        functools.partial(kernel, nblk, mems, bands),
+        functools.partial(kernel, mems, bands),
         out_shape=(
             jax.ShapeDtypeStruct(prior.shape, BF16),
             jax.ShapeDtypeStruct((capacity, SPAN), F32),
@@ -240,6 +263,7 @@
             pltpu.VMEM((pairs, members, PAIR), BF16),
             pltpu.VMEM((pairs, members, PAIR), BF16),
             pltpu.VMEM((BLOCKS, 2, members, SPAN), BF16),
+            pltpu.VMEM(taper.shape, F32),
             pltpu.VMEM((rim, members), BF16),
             pltpu.VMEM((members, rim), BF16),
             pltpu.VMEM((pairs, rim, PAIR), F32),
@@ -247,16 +271,15 @@
             pltpu.VMEM((rim, PAIR), F32),
             pltpu.VMEM((rim, PAIR), BF16),
             pltpu.VMEM((members, PAIR), F32),
-            pltpu.VMEM((pairs, PAIR), F32),
-            pltpu.VMEM((mems, pairs, PAIR), F32),
-            dma, dma, dma((4, 2)), dma((4, 2)), dma((pairs,)), dma, dma, dma, dma, dma,
+            pltpu.VMEM((per_worker, SPAN), F32),
+            pltpu.VMEM((mems, per_worker, SPAN), F32),
+            dma, dma, dma((4, 2 * members // CHUNK)), dma((4, 2 * members // CHUNK)), dma((pairs,)), dma, dma, dma, dma, dma,
         ],
         compiler_params=pltpu.CompilerParams(
             collective_id=0, has_side_effects=True, vmem_limit_bytes=60 << 20
         ),
     )(
-        rel.reshape(-1), fac.reshape(-1), table,
-        jnp.transpose(owner.reshape(patches // 2, 2)), prior, perturbed, solved,
+        jnp.transpose(groups), jnp.transpose(factors), taper, owner.reshape(1, patches), prior, perturbed, solved,
     )
 
 

time: 158 us -> 127 us (0.80)
  Pallas kernels: 145 us -> 119 us
  local copies, waits for them, and re-layouts: 10 us -> 5.09 us
    pallas_call x1, Pallas kernels: 145 us -> 119 us  [per_device(): pl.pallas_call(functools.partial(kernel, mems, bands), out_shape=(jax.Sha...]
    reshape x4 -> x0, local copies, waits for them, and re-layouts: 2.71 us -> none  [the longest x2 1.45 us: per_device(): owner.reshape(patches // 2, 2)]
    unnamed x5 -> x4, local copies, waits for them, and re-layouts: 7.12 us -> 5.09 us
where the time goes in v2:
time: 127 us; the launch traced here: 124 us
  Pallas kernels  119 us (94%)
  local copies, waits for them, and re-layouts  5.09 us (4%)
    pallas_call x1, Pallas kernels, per_device(): pl.pallas_call(functools.partial(kernel, mems, bands), out_shape=(jax.Sha...  119 us
    unnamed x4, local copies, waits for them, and re-layouts  5.09 us

profile of v2, /device:TPU:112, one launch (start us, length us, event | category | flops | bytes accessed | tf_op | source)
XLA Modules:
  0.0 124.4 jit_solution(1920497507017231454)
XLA Ops:
  0.6 118.7 %shard_map.86 = (bf16[64,32768]{1,0:T(8,128)(2,1)}, f32[32,128]{1,0:T(8,128)}) custom-call(s32[6,256]{1,0:T(8,128)} %bitcast.3, s32[6,256]{1,0:T(8,128)} %bitcast.4, f32[8,128,128]{2,1,0:T(8,128)} %taper.1, s32[1,256]{1,0:T(1,128)} %bitcast.5, bf16[64,32768]{1,0:T(8,128)(2,1)} %prior.1, bf16[64,2048]{1,0:T(8,128)(2,1)} %perturbed.1, bf16[64,2048]{1,0:T(8,128)(2,1)} %solved.1), custom_call_target="tpu_custom_call" | custom-call | tf_op jit(solution)/shard_map/pallas_call | solution.py:254
  119.3 0.0 copy-start
  119.3 4.5 %copy.11 = bf16[64,32768]{1,0:T(8,128)(2,1)} copy(bf16[64,32768]{1,0:T(8,128)(2,1)} %get-tuple-element.4) | data formatting | bytes 8388608
  123.8 0.0 copy-done
  123.8 0.6 copy.12
Async XLA Ops:
  119.3 4.5 %copy-start = (f32[32,128]{1,0:T(8,128)S(1)}, f32[32,128]{1,0:T(8,128)}, u32[]{:S(2)}) copy-start(f32[32,128]{1,0:T(8,128)} %get-tuple-element.5) | copy-start | bytes 49156

commit v3 on v2

--- a/solution.py
+++ b/solution.py
@@ -12,7 +12,9 @@
 SPAN = 128
 PAIR = 2 * SPAN
 SIDE = 4
-CHUNK = 128
+CHUNK = 512
+EARLY = 2
+AHEAD = 6
 F32 = jnp.float32
 BF16 = jnp.bfloat16
 MESH = pl.DeviceIdType.MESH
@@ -74,9 +76,9 @@
 
 def kernel(
     mems, bands,
-    groups, factors, taper, owner, prior, perturbed, solved,
+    groups_hbm, factors_hbm, taper_hbm, owner_hbm, prior, perturbed, solved,
     out, spread,
-    xbuf, ubuf, obs, table, ydt, s_all, weights, xd, cov, gain, inc, var_mine, var_all,
+    groups, factors, taper, owner, load_sem, xbuf, ubuf, obs, table, ydt, s_all, weights, xd, cov, gain, inc, var_mine, var_all,
     own_sem, own_send, near_recv, near_send, in_recv, in_send, out_recv, out_send, var_recv, var_send,
 ):
     band, me = lax.axis_index("band"), lax.axis_index("mem")
@@ -96,17 +98,76 @@
     right, left = chain(1), chain(-1)
 
     barrier = pltpu.get_barrier_semaphore()
-    for peer in peers:
+    for peer in reversed(peers):
         pl.semaphore_signal(barrier, inc=1, device_id={"mem": peer}, device_id_type=MESH)
     for peer in (left, right):
         pl.semaphore_signal(barrier, inc=1, device_id=peer, device_id_type=MESH)
-    pl.semaphore_wait(barrier, len(peers) + 2)
+    loads = [
+        pltpu.make_async_copy(source, target, load_sem.at[i])
+        for i, (source, target) in enumerate(
+            ((taper_hbm, taper), (groups_hbm, groups), (factors_hbm, factors), (owner_hbm, owner))
+        )
+    ]
+    for load in loads:
+        load.start()
 
     def columns(w, pair):
         return pl.ds(pl.multiple_of(w * width + pair * PAIR, PAIR), PAIR)
 
     def all_of(ref, sem):
         return pltpu.make_async_copy(ref, ref, sem)
+
+    def send_prior(pair, carry):
+        pltpu.make_async_copy(prior.at[:, columns(worker, pair)], xbuf.at[pair, rows, :], in_recv.at[pair]).start()
+        for peer in peers:
+            pltpu.make_async_remote_copy(
+                prior.at[:, columns(worker_of(band, peer), pair)], xbuf.at[pair, rows, :],
+                in_send, in_recv.at[pair], device_id={"mem": peer}, device_id_type=MESH,
+            ).start()
+        return carry
+
+    def make_weights(pair, carry):
+        pair_weights(
+            groups, factors, table, weights.at[pair], 2 * (worker * pairs + pair),
+            band * mems + worker - RIM, 1.0 / (members - 1),
+        )
+        return carry
+
+    def near_copy(source, target, slot, c, peer):
+        piece = pl.ds(pl.multiple_of((c % chunks) * CHUNK, CHUNK), CHUNK)
+        return pltpu.make_async_remote_copy(
+            obs.at[source, c // chunks, piece, :], obs.at[target, c // chunks, piece, :],
+            near_send.at[slot, c], near_recv.at[slot, c], device_id=peer, device_id_type=MESH,
+        )
+
+    chunks = members // CHUNK
+    steps = (
+        lambda c: near_copy(2, 1, 0, c, right), lambda c: near_copy(2, 3, 1, c, left),
+        lambda c: near_copy(1, 0, 2, c, right), lambda c: near_copy(3, 4, 3, c, left),
+    )
+
+    def near_first(c, carry):
+        steps[0](c).start()
+        steps[1](c).start()
+        return carry
+
+    def near_relay(c, carry):
+        for side in range(2):
+            steps[side](c).wait_recv()
+            steps[2 + side](c).start()
+        return carry
+
+    def near_last(c, carry):
+        steps[2](c).wait_recv()
+        steps[3](c).wait_recv()
+        return carry
+
+    def near_sent(c, carry):
+        for step in steps:
+            step(c).wait_send()
+        return carry
+
+    pl.semaphore_wait(barrier, len(peers) + 2)
 
     for i, source in enumerate((perturbed, solved)):
         pltpu.make_async_copy(
@@ -120,67 +181,18 @@
                 own_send, own_sem, device_id={"mem": peer}, device_id_type=MESH,
             ).start()
 
-    def send_prior(pair, carry):
-        pltpu.make_async_copy(prior.at[:, columns(worker, pair)], xbuf.at[pair, rows, :], in_recv.at[pair]).start()
-        for peer in peers:
-            pltpu.make_async_remote_copy(
-                prior.at[:, columns(worker_of(band, peer), pair)], xbuf.at[pair, rows, :],
-                in_send, in_recv.at[pair], device_id={"mem": peer}, device_id_type=MESH,
-            ).start()
-        return carry
-
-    def make_weights(pair, carry):
-        pair_weights(
-            groups, factors, table, weights.at[pair], 2 * (worker * pairs + pair),
-            band * mems + worker - RIM, 1.0 / (members - 1),
-        )
-        return carry
-
-    def near_copy(source, target, slot, c, peer):
-        piece = pl.ds(pl.multiple_of((c % chunks) * CHUNK, CHUNK), CHUNK)
-        return pltpu.make_async_remote_copy(
-            obs.at[source, c // chunks, piece, :], obs.at[target, c // chunks, piece, :],
-            near_send.at[slot, c], near_recv.at[slot, c], device_id=peer, device_id_type=MESH,
-        )
-
-    chunks = members // CHUNK
-    steps = (
-        lambda c: near_copy(2, 1, 0, c, right), lambda c: near_copy(2, 3, 1, c, left),
-        lambda c: near_copy(1, 0, 2, c, right), lambda c: near_copy(3, 4, 3, c, left),
-    )
-
-    def near_first(c, carry):
-        steps[0](c).start()
-        steps[1](c).start()
-        return carry
-
-    def near_relay(c, carry):
-        for side in range(2):
-            steps[side](c).wait_recv()
-            steps[2 + side](c).start()
-        return carry
-
-    def near_last(c, carry):
-        steps[2](c).wait_recv()
-        steps[3](c).wait_recv()
-        return carry
-
-    def near_sent(c, carry):
-        for step in steps:
-            step(c).wait_send()
-        return carry
-
     lax.fori_loop(0, 2, send_prior, 0)
+    for load in loads:
+        load.wait()
     for t in range(table.shape[0]):
         table[t] = jnp.transpose(taper[t])
-    lax.fori_loop(0, 2, make_weights, 0)
+    lax.fori_loop(0, EARLY, make_weights, 0)
     all_of(obs.at[RIM], own_sem).wait()
     lax.fori_loop(0, 2 * chunks, near_first, 0)
     lax.fori_loop(2, 4, send_prior, 0)
-    lax.fori_loop(2, 4, make_weights, 0)
     lax.fori_loop(0, 2 * chunks, near_relay, 0)
     lax.fori_loop(4, pairs, send_prior, 0)
-    lax.fori_loop(4, pairs, make_weights, 0)
+    lax.fori_loop(EARLY, pairs, make_weights, 0)
     lax.fori_loop(0, 2 * chunks, near_last, 0)
 
     for j in range(BLOCKS):
@@ -195,22 +207,31 @@
         for half in range(2):
             var_mine[pl.ds(2 * pair + half, 1), :] = var[:, half * SPAN:(half + 1) * SPAN]
         target = columns(worker, pair)
+
+        def send_back(some):
+            for peer in some:
+                theirs = pl.ds(pl.multiple_of(peer * local, local), local)
+                pltpu.make_async_remote_copy(
+                    ubuf.at[pair, theirs, :], out.at[:, target],
+                    out_send, out_recv, device_id={"mem": peer}, device_id_type=MESH,
+                ).start()
+
         pltpu.make_async_copy(ubuf.at[pair, rows, :], out.at[:, target], out_recv).start()
-        for peer in peers:
-            theirs = pl.ds(pl.multiple_of(peer * local, local), local)
-            pltpu.make_async_remote_copy(
-                ubuf.at[pair, theirs, :], out.at[:, target],
-                out_send, out_recv, device_id={"mem": peer}, device_id_type=MESH,
-            ).start()
-        return carry
-
+        send_back(back[:AHEAD])
+
+        @pl.when(pair == pairs - 1)
+        def _():
+            pltpu.make_async_copy(var_mine, var_all.at[worker], var_recv).start()
+            for peer in back:
+                pltpu.make_async_remote_copy(
+                    var_mine, var_all.at[worker], var_send, var_recv, device_id={"mem": peer}, device_id_type=MESH
+                ).start()
+
+        send_back(back[AHEAD:])
+        return carry
+
+    back = peers[::-1]
     lax.fori_loop(0, pairs, update, 0)
-
-    pltpu.make_async_copy(var_mine, var_all.at[worker], var_recv).start()
-    for peer in peers:
-        pltpu.make_async_remote_copy(
-            var_mine, var_all.at[worker], var_send, var_recv, device_id={"mem": peer}, device_id_type=MESH
-        ).start()
 
     mine = jnp.where(owner[...] == me, 1.0, 0.0).astype(F32)
     count = mine.shape[1]
@@ -246,9 +267,7 @@
     per_worker = patches // mems
     pairs = per_worker // 2
     capacity = 2 * per_worker
-    vmem = pl.BlockSpec(memory_space=pltpu.VMEM)
-    smem = pl.BlockSpec(memory_space=pltpu.SMEM)
-    hbm = pl.BlockSpec(memory_space=OUT_SPACE)
+    hbm = pl.BlockSpec(memory_space=pltpu.HBM)
     rim = BLOCKS * SPAN
     dma = pltpu.SemaphoreType.DMA
     return pl.pallas_call(
@@ -257,9 +276,14 @@
             jax.ShapeDtypeStruct(prior.shape, BF16),
             jax.ShapeDtypeStruct((capacity, SPAN), F32),
         ),
-        in_specs=[smem, smem, vmem, vmem] + [pl.BlockSpec(memory_space=pltpu.HBM)] * 3,
-        out_specs=(hbm, vmem),
+        in_specs=[hbm] * 7,
+        out_specs=(pl.BlockSpec(memory_space=OUT_SPACE), pl.BlockSpec(memory_space=pltpu.VMEM)),
         scratch_shapes=[
+            pltpu.SMEM(groups.shape[::-1], jnp.int32),
+            pltpu.SMEM(factors.shape[::-1], jnp.int32),
+            pltpu.VMEM(taper.shape, F32),
+            pltpu.VMEM((1, patches), jnp.int32),
+            dma((4,)),
             pltpu.VMEM((pairs, members, PAIR), BF16),
             pltpu.VMEM((pairs, members, PAIR), BF16),
             pltpu.VMEM((BLOCKS, 2, members, SPAN), BF16),
@@ -276,10 +300,12 @@
             dma, dma, dma((4, 2 * members // CHUNK)), dma((4, 2 * members // CHUNK)), dma((pairs,)), dma, dma, dma, dma, dma,
         ],
         compiler_params=pltpu.CompilerParams(
-            collective_id=0, has_side_effects=True, vmem_limit_bytes=60 << 20
+            collective_id=0, has_side_effects=True, vmem_limit_bytes=32 << 20
         ),
     )(
-        jnp.transpose(groups), jnp.transpose(factors), taper, owner.reshape(1, patches), prior, perturbed, solved,
+        *[pltpu.with_memory_space_constraint(a, pltpu.HBM) for a in (
+            jnp.transpose(groups), jnp.transpose(factors), taper, owner.reshape(1, patches), prior, perturbed, solved
+        )]
     )
 
 

time: 127 us -> 120 us (0.945)
  Pallas kernels: 119 us -> 115 us
  local copies, waits for them, and re-layouts: 5.09 us -> 2.62 us
    pallas_call x1, Pallas kernels: 119 us -> 115 us  [per_device(): pl.pallas_call(functools.partial(kernel, mems, bands), out_shape=(jax.Sha...]
    unnamed x4 -> x2, local copies, waits for them, and re-layouts: 5.09 us -> 2.62 us
where the time goes in v3:
time: 120 us; the launch traced here: 118 us
  Pallas kernels  115 us (96%)
  local copies, waits for them, and re-layouts  2.62 us (2%)
    pallas_call x1, Pallas kernels, per_device(): pl.pallas_call(functools.partial(kernel, mems, bands), out_shape=(jax.Sha...  115 us
    unnamed x2, local copies, waits for them, and re-layouts  2.62 us

profile of v3, /device:TPU:112, one launch (start us, length us, event | category | flops | bytes accessed | tf_op | source)
XLA Modules:
  0.0 118.3 jit_solution(15614450733490114502)
XLA Ops:
  0.6 115.1 %shard_map.86 = (bf16[64,32768]{1,0:T(8,128)(2,1)S(1)}, f32[32,128]{1,0:T(8,128)S(1)}) custom-call(s32[6,256]{1,0:T(8,128)} %bitcast.3, s32[6,256]{1,0:T(8,128)} %bitcast.4, f32[8,128,128]{2,1,0:T(8,128)} %taper_hbm.1, s32[1,256]{1,0:T(1,128)} %bitcast.5, bf16[64,32768]{1,0:T(8,128)(2,1)} %prior.1, bf16[64,2048]{1,0:T(8,128)(2,1)} %perturbed.1, ...), custom_call_target="tpu_custom_call" | custom-call | tf_op jit(solution)/shard_map/pallas_call | solution.py:273
  115.7 2.0 %copy.11 = bf16[64,32768]{1,0:T(8,128)(2,1)} copy(bf16[64,32768]{1,0:T(8,128)(2,1)S(1)} %get-tuple-element.4) | data formatting | bytes 8388608
  117.7 0.6 copy.12

commit v4 on v3

--- a/solution.py
+++ b/solution.py
@@ -15,6 +15,7 @@
 CHUNK = 512
 EARLY = 2
 AHEAD = 6
+PARTS = 8
 F32 = jnp.float32
 BF16 = jnp.bfloat16
 MESH = pl.DeviceIdType.MESH
@@ -259,6 +260,19 @@
     all_of(out, out_recv).wait()
 
 
+def store(analysis, spread, analysis_out, spread_out, sems):
+    rows = analysis.shape[0] // PARTS
+    copies = [
+        pltpu.make_async_copy(analysis.at[pl.ds(i * rows, rows), :], analysis_out.at[pl.ds(i * rows, rows), :], sems.at[i])
+        for i in range(PARTS)
+    ]
+    copies.append(pltpu.make_async_copy(spread, spread_out, sems.at[PARTS]))
+    for copy in copies:
+        copy.start()
+    for copy in copies:
+        copy.wait()
+
+
 def per_device(prior, perturbed, solved, taper, owner, groups, factors):
     mems, bands = lax.axis_size("mem"), lax.axis_size("band")
     local = prior.shape[0]
@@ -270,7 +284,7 @@
     hbm = pl.BlockSpec(memory_space=pltpu.HBM)
     rim = BLOCKS * SPAN
     dma = pltpu.SemaphoreType.DMA
-    return pl.pallas_call(
+    analysis, spread = pl.pallas_call(
         functools.partial(kernel, mems, bands),
         out_shape=(
             jax.ShapeDtypeStruct(prior.shape, BF16),
@@ -307,6 +321,17 @@
             jnp.transpose(groups), jnp.transpose(factors), taper, owner.reshape(1, patches), prior, perturbed, solved
         )]
     )
+    return pl.pallas_call(
+        store,
+        out_shape=(
+            jax.ShapeDtypeStruct(analysis.shape, analysis.dtype),
+            jax.ShapeDtypeStruct(spread.shape, spread.dtype),
+        ),
+        in_specs=[pl.BlockSpec(memory_space=pl.ANY)] * 2,
+        out_specs=(hbm, hbm),
+        scratch_shapes=[dma((PARTS + 1,))],
+        compiler_params=pltpu.CompilerParams(vmem_limit_bytes=1 << 20),
+    )(analysis, spread)
 
 
 OUT_SPACE = pltpu.HBM

time: 120 us -> 120 us (level)
  local copies, waits for them, and re-layouts: 2.62 us -> 0 us
  Pallas kernels: 115 us -> 117 us
    unnamed x2 -> x0, local copies, waits for them, and re-layouts: 2.62 us -> none
    pallas_call x0 -> x1, Pallas kernels: none -> 2.08 us  [per_device(): pl.pallas_call(store, out_shape=(jax.ShapeDtypeStruct(analysis.shape, ana...]
where the time goes in v4:
time: 120 us; the launch traced here: 118 us
  Pallas kernels  117 us (98%)
    pallas_call x1, Pallas kernels, per_device(): pl.pallas_call(functools.partial(kernel, mems, bands), out_shape=(jax.Sha...  115 us

profile of v4, /device:TPU:112, one launch (start us, length us, event | category | flops | bytes accessed | tf_op | source)
XLA Modules:
  0.0 117.8 jit_solution(11102589790489828703)
XLA Ops:
  0.6 115.1 %shard_map.86 = (bf16[64,32768]{1,0:T(8,128)(2,1)S(1)}, f32[32,128]{1,0:T(8,128)S(1)}) custom-call(s32[6,256]{1,0:T(8,128)} %bitcast.3, s32[6,256]{1,0:T(8,128)} %bitcast.4, f32[8,128,128]{2,1,0:T(8,128)} %taper_hbm.1, s32[1,256]{1,0:T(1,128)} %bitcast.5, bf16[64,32768]{1,0:T(8,128)(2,1)} %prior.1, bf16[64,2048]{1,0:T(8,128)(2,1)} %perturbed.1, ...), custom_call_target="tpu_custom_call" | custom-call | tf_op jit(solution)/shard_map/pallas_call | solution.py:287
  115.7 2.1 %shard_map.87 = (bf16[64,32768]{1,0:T(8,128)(2,1)}, f32[32,128]{1,0:T(8,128)}) custom-call(bf16[64,32768]{1,0:T(8,128)(2,1)S(1)} %get-tuple-element.4.analysis, f32[32,128]{1,0:T(8,128)S(1)} %get-tuple-element.5.spread), custom_call_target="tpu_custom_call" | custom-call | tf_op jit(solution)/shard_map/pallas_call | solution.py:324

commit v5 on v4

--- a/solution.py
+++ b/solution.py
@@ -19,7 +19,7 @@
 F32 = jnp.float32
 BF16 = jnp.bfloat16
 MESH = pl.DeviceIdType.MESH
-HOPS = ((0, 1), (1, 0), (0, 3), (3, 0), (1, 1), (3, 3), (1, 3), (3, 1), (0, 2), (2, 0), (1, 2), (2, 1), (3, 2), (2, 3), (2, 2))
+HOPS = ((0, 1), (1, 0), (0, 3), (3, 0), (0, 2), (1, 1), (3, 3), (1, 3), (3, 1), (2, 0), (2, 1), (1, 2), (2, 3), (3, 2), (2, 2))
 
 
 def pair_weights(groups, factors, table, w_ref, patch, first, scale):
@@ -119,12 +119,12 @@
         return pltpu.make_async_copy(ref, ref, sem)
 
     def send_prior(pair, carry):
-        pltpu.make_async_copy(prior.at[:, columns(worker, pair)], xbuf.at[pair, rows, :], in_recv.at[pair]).start()
         for peer in peers:
             pltpu.make_async_remote_copy(
                 prior.at[:, columns(worker_of(band, peer), pair)], xbuf.at[pair, rows, :],
                 in_send, in_recv.at[pair], device_id={"mem": peer}, device_id_type=MESH,
             ).start()
+        pltpu.make_async_copy(prior.at[:, columns(worker, pair)], xbuf.at[pair, rows, :], in_recv.at[pair]).start()
         return carry
 
     def make_weights(pair, carry):
@@ -217,7 +217,6 @@
                     out_send, out_recv, device_id={"mem": peer}, device_id_type=MESH,
                 ).start()
 
-        pltpu.make_async_copy(ubuf.at[pair, rows, :], out.at[:, target], out_recv).start()
         send_back(back[:AHEAD])
 
         @pl.when(pair == pairs - 1)
@@ -229,6 +228,7 @@
                 ).start()
 
         send_back(back[AHEAD:])
+        pltpu.make_async_copy(ubuf.at[pair, rows, :], out.at[:, target], out_recv).start()
         return carry
 
     back = peers[::-1]

time: 120 us -> 120 us (level)
  no operation moved by 1% of the time
where the time goes in v5:
time: 120 us; the launch traced here: 118 us
  Pallas kernels  117 us (98%)
    pallas_call x1, Pallas kernels, per_device(): pl.pallas_call(functools.partial(kernel, mems, bands), out_shape=(jax.Sha...  115 us

profile of v5, /device:TPU:112, one launch (start us, length us, event | category | flops | bytes accessed | tf_op | source)
XLA Modules:
  0.0 117.6 jit_solution(563724392961964290)
XLA Ops:
  0.6 114.9 %shard_map.86 = (bf16[64,32768]{1,0:T(8,128)(2,1)S(1)}, f32[32,128]{1,0:T(8,128)S(1)}) custom-call(s32[6,256]{1,0:T(8,128)} %bitcast.3, s32[6,256]{1,0:T(8,128)} %bitcast.4, f32[8,128,128]{2,1,0:T(8,128)} %taper_hbm.1, s32[1,256]{1,0:T(1,128)} %bitcast.5, bf16[64,32768]{1,0:T(8,128)(2,1)} %prior.1, bf16[64,2048]{1,0:T(8,128)(2,1)} %perturbed.1, ...), custom_call_target="tpu_custom_call" | custom-call | tf_op jit(solution)/shard_map/pallas_call | solution.py:287
  115.5 2.1 %shard_map.87 = (bf16[64,32768]{1,0:T(8,128)(2,1)}, f32[32,128]{1,0:T(8,128)}) custom-call(bf16[64,32768]{1,0:T(8,128)(2,1)S(1)} %get-tuple-element.4.analysis, f32[32,128]{1,0:T(8,128)S(1)} %get-tuple-element.5.spread), custom_call_target="tpu_custom_call" | custom-call | tf_op jit(solution)/shard_map/pallas_call | solution.py:324

commit v6 on v5

--- a/solution.py
+++ b/solution.py
@@ -79,7 +79,7 @@
     mems, bands,
     groups_hbm, factors_hbm, taper_hbm, owner_hbm, prior, perturbed, solved,
     out, spread,
-    groups, factors, taper, owner, load_sem, xbuf, ubuf, obs, table, ydt, s_all, weights, xd, cov, gain, inc, var_mine, var_all,
+    groups, factors, taper, owner, load_sem, var_f32, xbuf, ubuf, obs, table, ydt, s_all, weights, xd, cov, gain, inc, var_mine, var_all,
     own_sem, own_send, near_recv, near_send, in_recv, in_send, out_recv, out_send, var_recv, var_send,
 ):
     band, me = lax.axis_index("band"), lax.axis_index("mem")
@@ -206,7 +206,12 @@
         all_of(xbuf.at[pair], in_recv.at[pair]).wait()
         var = pair_update(xbuf.at[pair], ubuf.at[pair], ydt, s_all, weights.at[pair], xd, cov, gain, inc)
         for half in range(2):
-            var_mine[pl.ds(2 * pair + half, 1), :] = var[:, half * SPAN:(half + 1) * SPAN]
+            var_f32[pl.ds(2 * pair + half, 1), :] = var[:, half * SPAN:(half + 1) * SPAN]
+
+        @pl.when(pair == pairs - 1)
+        def _():
+            var_mine[...] = var_f32[...].astype(BF16)
+
         target = columns(worker, pair)
 
         def send_back(some):
@@ -248,7 +253,7 @@
     selector = jnp.where(slots == rank, 1.0, 0.0) * mine
     all_of(var_all, var_recv).wait()
     spread[...] = jnp.dot(
-        selector, var_all[...].reshape(count, SPAN), precision=lax.Precision.HIGHEST, preferred_element_type=F32
+        selector, var_all[...].astype(F32).reshape(count, SPAN), precision=lax.Precision.HIGHEST, preferred_element_type=F32
     )
 
     lax.fori_loop(0, 2 * chunks, near_sent, 0)
@@ -298,6 +303,7 @@
             pltpu.VMEM(taper.shape, F32),
             pltpu.VMEM((1, patches), jnp.int32),
             dma((4,)),
+            pltpu.VMEM((per_worker, SPAN), F32),
             pltpu.VMEM((pairs, members, PAIR), BF16),
             pltpu.VMEM((pairs, members, PAIR), BF16),
             pltpu.VMEM((BLOCKS, 2, members, SPAN), BF16),
@@ -309,8 +315,8 @@
             pltpu.VMEM((rim, PAIR), F32),
             pltpu.VMEM((rim, PAIR), BF16),
             pltpu.VMEM((members, PAIR), F32),
-            pltpu.VMEM((per_worker, SPAN), F32),
-            pltpu.VMEM((mems, per_worker, SPAN), F32),
+            pltpu.VMEM((per_worker, SPAN), BF16),
+            pltpu.VMEM((mems, per_worker, SPAN), BF16),
             dma, dma, dma((4, 2 * members // CHUNK)), dma((4, 2 * members // CHUNK)), dma((pairs,)), dma, dma, dma, dma, dma,
         ],
         compiler_params=pltpu.CompilerParams(

time: 120 us -> 119 us (level)
  no operation moved by 1% of the time
where the time goes in v6:
time: 119 us; the launch traced here: 117 us
  Pallas kernels  116 us (97%)
    pallas_call x1, Pallas kernels, per_device(): pl.pallas_call(functools.partial(kernel, mems, bands), out_shape=(jax.Sha...  114 us

profile of v6, /device:TPU:112, one launch (start us, length us, event | category | flops | bytes accessed | tf_op | source)
XLA Modules:
  0.0 116.9 jit_solution(6994740221476019743)
XLA Ops:
  0.6 114.1 %shard_map.86 = (bf16[64,32768]{1,0:T(8,128)(2,1)S(1)}, f32[32,128]{1,0:T(8,128)S(1)}) custom-call(s32[6,256]{1,0:T(8,128)} %bitcast.3, s32[6,256]{1,0:T(8,128)} %bitcast.4, f32[8,128,128]{2,1,0:T(8,128)} %taper_hbm.1, s32[1,256]{1,0:T(1,128)} %bitcast.5, bf16[64,32768]{1,0:T(8,128)(2,1)} %prior.1, bf16[64,2048]{1,0:T(8,128)(2,1)} %perturbed.1, ...), custom_call_target="tpu_custom_call" | custom-call | tf_op jit(solution)/shard_map/pallas_call | solution.py:292
  114.8 2.1 %shard_map.87 = (bf16[64,32768]{1,0:T(8,128)(2,1)}, f32[32,128]{1,0:T(8,128)}) custom-call(bf16[64,32768]{1,0:T(8,128)(2,1)S(1)} %get-tuple-element.4.analysis, f32[32,128]{1,0:T(8,128)S(1)} %get-tuple-element.5.spread), custom_call_target="tpu_custom_call" | custom-call | tf_op jit(solution)/shard_map/pallas_call | solution.py:330
